TPU v7x, 256 devices: a whole 4x4x8 slice. The times are simulated.
256 devices in a mesh: leaf: 16 (over y, x), col: 16 (over z, core).
Axes of the slice: x: 4, y: 4, z: 8, core: 2. Of those that a mesh axis runs over, the one named last changes fastest.
Arguments:
- right_sides: bfloat16 [16, 2, 1792, 128], P('leaf', None, 'col'), may hold values from -6 to 6
- leaf_inverse: bfloat16 [16, 1792, 1792], P('leaf', 'col'), as said below
- upper_inverse: bfloat16 [16, 1792, 1792], P('leaf', 'col'), as said below
- leaf_update: bfloat16 [16, 4, 1792, 512], P('leaf', None, 'col'), may hold values from -0.0625 to 0.0625
- upper_update: bfloat16 [16, 4, 1792, 512], P('leaf', None, 'col'), may hold values from -0.0625 to 0.0625
- live_rows: int32 [16, 2], P('leaf'), may hold values from 896 to 1792, as said below
- tile_map: int32 [16, 2, 4, 512], P('leaf'), may hold values from 0 to 1791, as said below
Outputs:
- solution: bfloat16 [16, 2, 1792, 128], P('leaf', None, 'col')
Inputs may be any that keep to these rules, and one draw needn't show every extreme that they name: `leaf_inverse`: zero above the diagonal, nonzero on it. `upper_inverse`: zero above the diagonal, nonzero on it. `live_rows`: one supernode has all 1792 rows live and one has 896. `tile_map`: the rows of one tile are distinct and increasing.
All inputs are finite; a program needn't handle non-finite values.
Results may differ from a plain program's by a relative error of at most 0.0075.
Values may be sent and summed in bfloat16 or wider, within the bound.
No kernel may reach another device: no remote copies, remote signals or barrier semaphores. Data moves between devices by JAX's collectives and lax.ppermute only.
A program may use at most 64 MiB of HBM per device.

v0:
```python
import jax
import jax.numpy as jnp
from jax import lax
from jax.sharding import PartitionSpec as P


def forward_solve(inverse_rows, residual, row_mask, active):
    shares = (residual * row_mask).astype(jnp.bfloat16)
    empty = jnp.zeros((inverse_rows.shape[0], residual.shape[1]), jnp.float32)
    shard_rows = lax.all_gather(shares, "col", axis=0, tiled=True)
    solved = lax.cond(
        active,
        lambda: jnp.dot(inverse_rows, shard_rows, preferred_element_type=jnp.float32),
        lambda: empty,
    )
    return (solved * row_mask).astype(jnp.bfloat16)


def tile_terms(update_cols, solved, active):

    def tile_compute():
        return jnp.einsum("srt,rn->stn", update_cols, solved, preferred_element_type=jnp.float32)

    def tile_nothing():
        return jnp.zeros((update_cols.shape[0], update_cols.shape[2], solved.shape[1]), jnp.float32)

    local_terms = lax.cond(active, tile_compute, tile_nothing)
    return lax.psum(local_terms, "col")


def spread(summed, tile_rows, first_row, rows_dev):
    local_rows = tile_rows - first_row
    inside = (local_rows >= 0) & (local_rows < rows_dev)
    target = jnp.where(inside, local_rows, rows_dev)

    def one_slot(values, where_to):
        return (
            jnp.zeros((rows_dev, values.shape[1]), jnp.float32)
            .at[where_to]
            .add(values, mode="drop")
        )

    return jax.vmap(one_slot)(summed, target)


def pick_rows(fetched, tile_rows, first_row, rows_dev):
    local_rows = tile_rows - first_row
    inside = (local_rows >= 0) & (local_rows < rows_dev)
    chosen = fetched[jnp.clip(local_rows, 0, rows_dev - 1)]
    return jnp.where(inside[:, None], chosen, jnp.zeros_like(chosen))


def backward_solve(inverse_rows, solved, pulled, row_mask, active):
    scaled = ((solved.astype(jnp.float32) - pulled) * row_mask).astype(jnp.bfloat16)
    rhs_width = scaled.shape[1]
    row_count = inverse_rows.shape[0] * lax.axis_size("col")

    def rows_compute():
        return lax.dot_general(
            inverse_rows, scaled, (((0,), (0,)), ((), ())), preferred_element_type=jnp.float32
        )

    summed = lax.psum_scatter(
        lax.cond(active, rows_compute, lambda: jnp.zeros((row_count, rhs_width), jnp.float32)),
        "col",
        scatter_dimension=0,
        tiled=True,
    )
    return (summed * row_mask).astype(jnp.bfloat16)


def pull_terms(update_cols, tiles, active):

    def pull_compute():
        return jnp.einsum("srt,stn->rn", update_cols, tiles, preferred_element_type=jnp.float32)

    def pull_nothing():
        return jnp.zeros((update_cols.shape[1], tiles.shape[2]), jnp.float32)

    return lax.cond(active, pull_compute, pull_nothing)


def deliver(outgoing, height, leaf_id, leaf_count):
    owner = leaf_id // 2**height * 2**height + 2 ** (height - 1)
    onehot = (jnp.arange(leaf_count, dtype=jnp.int32) == owner).astype(jnp.float32)
    slot_table = onehot[:, None, None] * outgoing[None]
    return lax.psum_scatter(slot_table, "leaf", scatter_dimension=0, tiled=True)[0]


def fetch(answer_up, height, leaf_id):
    owner = leaf_id // 2**height * 2**height + 2 ** (height - 1)
    gathered = lax.all_gather(answer_up[None], "leaf", axis=0, tiled=True)
    return lax.dynamic_index_in_dim(gathered, owner, 0, keepdims=False)


def shards(
    right_sides, leaf_inverse, upper_inverse, leaf_update, upper_update, live_rows, tile_map
):
    leaf_count = lax.axis_size("leaf")
    depth = leaf_count.bit_length() - 1
    rows_dev = leaf_inverse.shape[1]
    rhs_width = right_sides.shape[3]
    tile_len = tile_map.shape[3]
    leaf_id = lax.axis_index("leaf")
    col_id = lax.axis_index("col")
    first_row = col_id * rows_dev
    row_ids = first_row + jnp.arange(rows_dev, dtype=jnp.int32)
    leaf_mask = (row_ids < live_rows[0, 0]).astype(jnp.float32)[:, None]
    upper_mask = (row_ids < live_rows[0, 1]).astype(jnp.float32)[:, None]
    node_level = jnp.zeros((), jnp.int32)
    for height in range(1, depth + 1):
        node_level = node_level + ((leaf_id % 2 ** (height - 1) == 0) & (leaf_id > 0)).astype(
            jnp.int32
        )
    always = jnp.array(True)
    solved_leaf = forward_solve(
        leaf_inverse[0], right_sides[0, 0].astype(jnp.float32), leaf_mask, always
    )
    summed = tile_terms(leaf_update[0, :depth], solved_leaf, always)
    pieces = spread(summed, tile_map[0, 0, :depth], first_row, rows_dev)
    outgoing = [None] + [pieces[height - 1] for height in range(1, depth + 1)]
    residual_up = right_sides[0, 1].astype(jnp.float32)
    solved_up = jnp.zeros((rows_dev, rhs_width), jnp.bfloat16)
    for height in range(1, depth + 1):
        residual_up = residual_up - deliver(outgoing[height], height, leaf_id, leaf_count)
        active = node_level == height
        solved = forward_solve(upper_inverse[0], residual_up, upper_mask, active)
        solved_up = jnp.where(active, solved, solved_up)
        slot_count = depth - height
        if slot_count > 0:
            summed = tile_terms(upper_update[0, :slot_count], solved, active)
            pieces = spread(summed, tile_map[0, 1, :slot_count], first_row, rows_dev)
            for slot_idx in range(slot_count):
                outgoing[height + 1 + slot_idx] = outgoing[height + 1 + slot_idx] + pieces[slot_idx]
    answer_up = jnp.zeros((rows_dev, rhs_width), jnp.bfloat16)
    tiles_leaf = [None] * depth
    tiles_upper = jnp.zeros((depth, tile_len, rhs_width), jnp.bfloat16)
    for height in range(depth, 0, -1):
        active = node_level == height
        slot_count = depth - height
        if slot_count > 0:
            pulled = pull_terms(upper_update[0, :slot_count], tiles_upper[:slot_count], active)
        else:
            pulled = jnp.zeros((rows_dev, rhs_width), jnp.float32)
        answer = backward_solve(upper_inverse[0], solved_up, pulled, upper_mask, active)
        answer_up = jnp.where(active, answer, answer_up)
        fetched = fetch(answer_up, height, leaf_id)
        slot_now = jnp.clip(height - node_level - 1, 0, depth - 1)
        valid = (node_level > 0) & (node_level < height)
        upper_map = lax.dynamic_index_in_dim(tile_map[0, 1], slot_now, 0, keepdims=False)
        leaf_part = pick_rows(fetched, tile_map[0, 0, height - 1], first_row, rows_dev)
        upper_part = pick_rows(fetched, upper_map, first_row, rows_dev)
        upper_part = jnp.where(valid, upper_part, jnp.zeros_like(upper_part))
        both = (
            lax.psum(jnp.stack([leaf_part, upper_part]), "col")
            .astype(jnp.float32)
            .astype(jnp.bfloat16)
        )
        tiles_leaf[height - 1] = both[0]
        updated = lax.dynamic_update_index_in_dim(tiles_upper, both[1], slot_now, 0)
        tiles_upper = jnp.where(valid, updated, tiles_upper)
    pulled = pull_terms(leaf_update[0, :depth], jnp.stack(tiles_leaf), always)
    answer_leaf = backward_solve(leaf_inverse[0], solved_leaf, pulled, leaf_mask, always)
    return jnp.stack([answer_leaf, answer_up])[None]


def solution(mesh):
    placed = (
        P("leaf", None, "col", None),
        P("leaf", "col", None),
        P("leaf", "col", None),
        P("leaf", None, "col", None),
        P("leaf", None, "col", None),
        P("leaf", None),
        P("leaf", None, None, None),
    )
    return jax.shard_map(
        shards, mesh=mesh, in_specs=placed, out_specs=P("leaf", None, "col", None), check_vma=False
    )
```

profile of v0, /device:TPU:4, one launch (start us, length us, event | category | flops | bytes accessed | tf_op | source)
XLA Modules:
  0.0 1755.9 jit_solution(690837087671866343)
XLA Ops:
  6.5 1.4 fusion.78
  9.4 21.2 %all_gather.27 = bf16[1792,128]{1,0:T(8,128)(2,1)S(1)} all-gather(bf16[112,128]{1,0:T(8,128)(2,1)S(1)} %fusion.53), channel_id=1, replica_groups=mesh['leaf'=16,'col'=16] {'col'}, dimensions={0}, use_global_device_ids=true | all-gather | bytes 487424 | tf_op jit(solution)/shard_map/all_gather | solution.py:10
  34.5 108.2 %all-reduce.13.cloned.1.call-done = f32[4,512,128]{1,2,0:T(8,128)} async-done(((f32[4,512,128]{1,2,0:T(8,128)}), f32[4,512,128]{1,2,0:T(8,128)}) %all-reduce.13.cloned.1.call-update) | async-done | bytes 1048592 | tf_op jit(solution)/shard_map/psum | solution.py:28
  142.7 1.5 copy.73
  144.3 11.5 scatter_custom_fusion.1
  158.6 77.5 %reduce-scatter.38.cloned.1.call-done = f32[1,112,128]{2,1,0:T(8,128)} async-done(((f32[16,112,128]{2,1,0:T(8,128)}), f32[1,112,128]{2,1,0:T(8,128)}) %reduce-scatter.38.cloned.1.call-update) | async-done | bytes 57360
  237.0 18.7 %all_gather.28 = bf16[1792,128]{1,0:T(8,128)(2,1)S(1)} all-gather(bf16[112,128]{1,0:T(8,128)(2,1)S(1)} %multiply_convert_fusion.11), channel_id=1, replica_groups=mesh['leaf'=16,'col'=16] {'col'}, dimensions={0}, use_global_device_ids=true | all-gather | bytes 487424 | tf_op jit(solution)/shard_map/all_gather | solution.py:10
  257.0 109.0 %all-reduce.15.cloned.1.call-done = f32[3,512,128]{2,1,0:T(8,128)} async-done(((f32[3,512,128]{2,1,0:T(8,128)}), f32[3,512,128]{2,1,0:T(8,128)}) %all-reduce.15.cloned.1.call-update) | async-done | bytes 786448 | tf_op jit(solution)/shard_map/psum | solution.py:28
  366.0 9.1 scatter_custom_fusion.2
  377.1 78.3 %reduce-scatter.40.cloned.1.call-done = f32[1,112,128]{2,1,0:T(8,128)} async-done(((f32[16,112,128]{2,1,0:T(8,128)}), f32[1,112,128]{2,1,0:T(8,128)}) %reduce-scatter.40.cloned.1.call-update) | async-done | bytes 57360
  456.3 18.7 %all_gather.29 = bf16[1792,128]{1,0:T(8,128)(2,1)S(1)} all-gather(bf16[112,128]{1,0:T(8,128)(2,1)S(1)} %get-tuple-element.234), channel_id=1, replica_groups=mesh['leaf'=16,'col'=16] {'col'}, dimensions={0}, use_global_device_ids=true | all-gather | bytes 487424 | tf_op jit(solution)/shard_map/all_gather | solution.py:10
  476.6 107.9 %all-reduce.17.cloned.1.call-done = f32[2,512,128]{2,1,0:T(8,128)} async-done(((f32[2,512,128]{2,1,0:T(8,128)}), f32[2,512,128]{2,1,0:T(8,128)}) %all-reduce.17.cloned.1.call-update) | async-done | bytes 524304 | tf_op jit(solution)/shard_map/psum | solution.py:28
  584.4 6.4 scatter_custom_fusion.3
  592.1 79.1 %reduce-scatter.42.cloned.1.call-done = f32[1,112,128]{2,1,0:T(8,128)} async-done(((f32[16,112,128]{2,1,0:T(8,128)}), f32[1,112,128]{2,1,0:T(8,128)}) %reduce-scatter.42.cloned.1.call-update) | async-done | bytes 57360
  672.2 18.7 %all_gather.30 = bf16[1792,128]{1,0:T(8,128)(2,1)S(1)} all-gather(bf16[112,128]{1,0:T(8,128)(2,1)S(1)} %multiply_convert_fusion.7), channel_id=1, replica_groups=mesh['leaf'=16,'col'=16] {'col'}, dimensions={0}, use_global_device_ids=true | all-gather | bytes 487424 | tf_op jit(solution)/shard_map/all_gather | solution.py:10
  691.8 106.9 %all-reduce.19.cloned.1.call-done = f32[1,512,128]{2,1,0:T(8,128)} async-done(((f32[1,512,128]{2,1,0:T(8,128)}), f32[1,512,128]{2,1,0:T(8,128)}) %all-reduce.19.cloned.1.call-update) | async-done | bytes 262160 | tf_op jit(solution)/shard_map/psum | solution.py:28
  798.7 3.9 scatter_custom_fusion
  803.8 79.3 %reduce-scatter.44.cloned.1.call-done = f32[1,112,128]{2,1,0:T(8,128)} async-done(((f32[16,112,128]{2,1,0:T(8,128)}), f32[1,112,128]{2,1,0:T(8,128)}) %reduce-scatter.44.cloned.1.call-update) | async-done | bytes 57360
  884.0 18.7 %all_gather.31 = bf16[1792,128]{1,0:T(8,128)(2,1)S(1)} all-gather(bf16[112,128]{1,0:T(8,128)(2,1)S(1)} %fusion.55), channel_id=1, replica_groups=mesh['leaf'=16,'col'=16] {'col'}, dimensions={0}, use_global_device_ids=true | all-gather | bytes 487424 | tf_op jit(solution)/shard_map/all_gather | solution.py:10
  906.3 52.8 %reduce-scatter.28.cloned.1.call-done = f32[112,128]{1,0:T(8,128)} async-done(((f32[1792,128]{1,0:T(8,128)}), f32[112,128]{1,0:T(8,128)}) %reduce-scatter.28.cloned.1.call-update) | async-done | bytes 57360 | tf_op jit(solution)/shard_map/reduce_scatter | solution.py:63
  960.0 23.5 %all-gather = bf16[1792,128]{1,0:T(8,128)(2,1)S(1)} all-gather(bf16[112,128]{1,0:T(8,128)(2,1)S(1)} %fusion.60), channel_id=2, replica_groups=mesh['leaf'=16,'col'=16] {'leaf'}, dimensions={0}, use_global_device_ids=true | all-gather | bytes 487424 | tf_op jit(solution)/shard_map/all_gather | solution.py:92
  987.3 107.1 %all-reduce.21.cloned.1.call-done = bf16[2,512,128]{2,1,0:T(8,128)(2,1)} async-done(((bf16[2,512,128]{2,1,0:T(8,128)(2,1)}), bf16[2,512,128]{2,1,0:T(8,128)(2,1)}) %all-reduce.21.cloned.1.call-update) | async-done | bytes 262160 | tf_op jit(solution)/shard_map/psum | solution.py:155
  1096.6 58.6 %reduce-scatter.30.cloned.1.call-done = f32[112,128]{1,0:T(8,128)} async-done(((f32[1792,128]{1,0:T(8,128)}), f32[112,128]{1,0:T(8,128)}) %reduce-scatter.30.cloned.1.call-update) | async-done | bytes 57360 | tf_op jit(solution)/shard_map/reduce_scatter | solution.py:63
  1156.2 23.6 %all-gather.1 = bf16[1792,128]{1,0:T(8,128)(2,1)S(1)} all-gather(bf16[112,128]{1,0:T(8,128)(2,1)S(1)} %fusion.61), channel_id=3, replica_groups=mesh['leaf'=16,'col'=16] {'leaf'}, dimensions={0}, use_global_device_ids=true | all-gather | bytes 487424 | tf_op jit(solution)/shard_map/all_gather | solution.py:92
  1183.5 107.0 %all-reduce.23.cloned.1.call-done = bf16[2,512,128]{2,1,0:T(8,128)(2,1)} async-done(((bf16[2,512,128]{2,1,0:T(8,128)(2,1)}), bf16[2,512,128]{2,1,0:T(8,128)(2,1)}) %all-reduce.23.cloned.1.call-update) | async-done | bytes 262160 | tf_op jit(solution)/shard_map/psum | solution.py:155
  1293.9 58.4 %reduce-scatter.32.cloned.1.call-done = f32[112,128]{1,0:T(8,128)} async-done(((f32[1792,128]{1,0:T(8,128)}), f32[112,128]{1,0:T(8,128)}) %reduce-scatter.32.cloned.1.call-update) | async-done | bytes 57360 | tf_op jit(solution)/shard_map/reduce_scatter | solution.py:63
  1353.1 23.6 %all-gather.2 = bf16[1792,128]{1,0:T(8,128)(2,1)S(1)} all-gather(bf16[112,128]{1,0:T(8,128)(2,1)S(1)} %fusion.62), channel_id=4, replica_groups=mesh['leaf'=16,'col'=16] {'leaf'}, dimensions={0}, use_global_device_ids=true | all-gather | bytes 487424 | tf_op jit(solution)/shard_map/all_gather | solution.py:92
  1381.7 107.2 %all-reduce.25.cloned.1.call-done = bf16[2,512,128]{2,1,0:T(8,128)(2,1)} async-done(((bf16[2,512,128]{2,1,0:T(8,128)(2,1)}), bf16[2,512,128]{2,1,0:T(8,128)(2,1)}) %all-reduce.25.cloned.1.call-update) | async-done | bytes 262160 | tf_op jit(solution)/shard_map/psum | solution.py:155
  1491.0 58.9 %reduce-scatter.34.cloned.1.call-done = f32[112,128]{1,0:T(8,128)} async-done(((f32[1792,128]{1,0:T(8,128)}), f32[112,128]{1,0:T(8,128)}) %reduce-scatter.34.cloned.1.call-update) | async-done | bytes 57360 | tf_op jit(solution)/shard_map/reduce_scatter | solution.py:63
  1550.7 23.6 %all-gather.3 = bf16[1792,128]{1,0:T(8,128)(2,1)S(1)} all-gather(bf16[112,128]{1,0:T(8,128)(2,1)S(1)} %fusion.63), channel_id=5, replica_groups=mesh['leaf'=16,'col'=16] {'leaf'}, dimensions={0}, use_global_device_ids=true | all-gather | bytes 487424 | tf_op jit(solution)/shard_map/all_gather | solution.py:92
  1580.2 106.1 %all-reduce.27.cloned.1.call-done = bf16[2,512,128]{2,1,0:T(8,128)(2,1)} async-done(((bf16[2,512,128]{2,1,0:T(8,128)(2,1)}), bf16[2,512,128]{2,1,0:T(8,128)(2,1)}) %all-reduce.27.cloned.1.call-update) | async-done | bytes 262160 | tf_op jit(solution)/shard_map/psum | solution.py:155
  1689.1 58.7 %reduce-scatter.36.cloned.1.call-done = f32[112,128]{1,0:T(8,128)} async-done(((f32[1792,128]{1,0:T(8,128)}), f32[112,128]{1,0:T(8,128)}) %reduce-scatter.36.cloned.1.call-update) | async-done | bytes 57360 | tf_op jit(solution)/shard_map/reduce_scatter | solution.py:63
  (233 shorter events, 57.5 us)
Async XLA Ops:
  6.5 24.4 %copy-start = (bf16[1,4,112,512]{3,2,1,0:T(8,128)(2,1)S(1)}, bf16[1,4,112,512]{3,2,1,0:T(8,128)(2,1)}, u32[]{:S(2)}) copy-start(bf16[1,4,112,512]{3,2,1,0:T(8,128)(2,1)} %param.38) | copy-start | bytes 1376260
  6.5 24.1 %copy-start.8 = (bf16[1,112,1792]{2,1,0:T(8,128)(2,1)S(1)}, bf16[1,112,1792]{2,1,0:T(8,128)(2,1)}, u32[]{:S(2)}) copy-start(bf16[1,112,1792]{2,1,0:T(8,128)(2,1)} %param.36) | copy-start | bytes 1204228
  6.5 136.2 %all-reduce.13.cloned.1.call-start = ((), (), s32[]{:S(2)}) async-start(), calls=%async_computation.9 | async-start | bytes 2097152 | tf_op jit(solution)/shard_map/psum | solution.py:28
  31.0 1.3 copy-start.16
  32.3 203.8 %reduce-scatter.38.cloned.1.call-start = ((), (), s32[]{:S(2)}) async-start(), calls=%async_computation.22 | async-start | bytes 974848
  156.9 1.6 copy-start.10
  156.9 209.0 %all-reduce.15.cloned.1.call-start = ((), (), s32[]{:S(2)}) async-start(), calls=%async_computation.10 | async-start | bytes 1572864 | tf_op jit(solution)/shard_map/psum | solution.py:28
  158.5 77.6 %copy-start.24 = (bf16[1,2,112,128]{3,2,1,0:T(8,128)(2,1)S(1)}, bf16[1,2,112,128]{3,2,1,0:T(8,128)(2,1)}, u32[]{:S(2)}) copy-start(bf16[1,2,112,128]{3,2,1,0:T(8,128)(2,1)} %param.35) | copy-start | bytes 172036
  158.6 97.1 %copy-start.1 = (bf16[1,112,1792]{2,1,0:T(8,128)(2,1)S(1)}, bf16[1,112,1792]{2,1,0:T(8,128)(2,1)}, u32[]{:S(2)}) copy-start(bf16[1,112,1792]{2,1,0:T(8,128)(2,1)} %param.37) | copy-start | bytes 1204228
  256.8 198.6 %reduce-scatter.40.cloned.1.call-start = ((), (), s32[]{:S(2)}) async-start(), calls=%async_computation.23 | async-start | bytes 974848
  376.2 208.2 %all-reduce.17.cloned.1.call-start = ((), (), s32[]{:S(2)}) async-start(), calls=%async_computation.11 | async-start | bytes 1048576 | tf_op jit(solution)/shard_map/psum | solution.py:28
  377.1 78.4 %copy-start.20 = (f32[1,112,128]{2,1,0:T(8,128)S(1)}, f32[1,112,128]{2,1,0:T(8,128)}, u32[]{:S(2)}) copy-start(f32[1,112,128]{2,1,0:T(8,128)} %reduce-scatter.38.cloned.1.call-done) | copy-start | bytes 172036
  476.5 194.8 %reduce-scatter.42.cloned.1.call-start = ((), (), s32[]{:S(2)}) async-start(), calls=%async_computation.24 | async-start | bytes 974848
  592.0 206.7 %all-reduce.19.cloned.1.call-start = ((), (), s32[]{:S(2)}) async-start(), calls=%async_computation.12 | async-start | bytes 524288 | tf_op jit(solution)/shard_map/psum | solution.py:28
  691.7 191.4 %reduce-scatter.44.cloned.1.call-start = ((), (), s32[]{:S(2)}) async-start(), calls=%async_computation.25 | async-start | bytes 974848
  803.7 79.4 %copy-start.22 = (f32[1,112,128]{2,1,0:T(8,128)S(1)}, f32[1,112,128]{2,1,0:T(8,128)}, u32[]{:S(2)}) copy-start(f32[1,112,128]{2,1,0:T(8,128)} %reduce-scatter.42.cloned.1.call-done) | copy-start | bytes 172036
  803.7 155.4 %reduce-scatter.28.cloned.1.call-start = ((), (), s32[]{:S(2)}) async-start(), calls=%async_computation.17 | async-start | bytes 974848 | tf_op jit(solution)/shard_map/reduce_scatter | solution.py:63
  902.8 192.6 %copy-start.11 = (bf16[112,128]{1,0:T(8,128)(2,1)}, bf16[112,128]{1,0:T(8,128)(2,1)S(1)}, u32[]{:S(2)}) copy-start(bf16[112,128]{1,0:T(8,128)(2,1)S(1)} %get-tuple-element.233) | copy-start | bytes 86020
  903.8 190.5 %all-reduce.21.cloned.1.call-start = ((), (), s32[]{:S(2)}) async-start(), calls=%async_computation.13 | async-start | bytes 524288 | tf_op jit(solution)/shard_map/psum | solution.py:155
  987.2 168.0 %reduce-scatter.30.cloned.1.call-start = ((), (), s32[]{:S(2)}) async-start(), calls=%async_computation.18 | async-start | bytes 974848 | tf_op jit(solution)/shard_map/reduce_scatter | solution.py:63
  1095.6 59.7 %copy-start.21 = (f32[112,128]{1,0:T(8,128)S(1)}, f32[112,128]{1,0:T(8,128)}, u32[]{:S(2)}) copy-start(f32[112,128]{1,0:T(8,128)} %reduce-scatter.28.cloned.1.call-done) | copy-start | bytes 172036
  1096.5 194.1 %all-reduce.23.cloned.1.call-start = ((), (), s32[]{:S(2)}) async-start(), calls=%async_computation.14 | async-start | bytes 524288 | tf_op jit(solution)/shard_map/psum | solution.py:155
  1156.1 23.6 %copy-start.18 = (bf16[112,128]{1,0:T(8,128)(2,1)}, bf16[112,128]{1,0:T(8,128)(2,1)S(1)}, u32[]{:S(2)}) copy-start(bf16[112,128]{1,0:T(8,128)(2,1)S(1)} %fusion.61) | copy-start | bytes 86020
  1183.5 168.7 %reduce-scatter.32.cloned.1.call-start = ((), (), s32[]{:S(2)}) async-start(), calls=%async_computation.19 | async-start | bytes 974848 | tf_op jit(solution)/shard_map/reduce_scatter | solution.py:63
  1292.8 1.0 copy-start.26
  1292.8 1.1 copy-start.25
  1293.7 58.5 %copy-start.19 = (bf16[112,128]{1,0:T(8,128)(2,1)S(1)}, bf16[112,128]{1,0:T(8,128)(2,1)}, u32[]{:S(2)}) copy-start(bf16[112,128]{1,0:T(8,128)(2,1)} %copy-done.18) | copy-start | bytes 86020
  1293.8 195.2 %all-reduce.25.cloned.1.call-start = ((), (), s32[]{:S(2)}) async-start(), calls=%async_computation.15 | async-start | bytes 524288 | tf_op jit(solution)/shard_map/psum | solution.py:155
  1381.7 168.1 %reduce-scatter.34.cloned.1.call-start = ((), (), s32[]{:S(2)}) async-start(), calls=%async_computation.20 | async-start | bytes 974848 | tf_op jit(solution)/shard_map/reduce_scatter | solution.py:63
  1490.9 195.5 %all-reduce.27.cloned.1.call-start = ((), (), s32[]{:S(2)}) async-start(), calls=%async_computation.16 | async-start | bytes 524288 | tf_op jit(solution)/shard_map/psum | solution.py:155
  1579.3 168.5 %reduce-scatter.36.cloned.1.call-start = ((), (), s32[]{:S(2)}) async-start(), calls=%async_computation.21 | async-start | bytes 974848 | tf_op jit(solution)/shard_map/reduce_scatter | solution.py:63
  1580.2 106.1 %copy-start.17 = (bf16[128,112]{0,1:T(8,128)(2,1)S(1)}, bf16[128,112]{0,1:T(8,128)(2,1)}, u32[]{:S(2)}) copy-start(bf16[128,112]{0,1:T(8,128)(2,1)} %copy-done.16) | copy-start | bytes 86020
  (21 other events, 16.3 us)
Sparse Core Ops, SparseCore 0:
  32.4 110.2 all-reduce.12
  157.1 78.9 reduce-scatter.37
  256.9 108.9 all-reduce.14
  376.3 79.0 reduce-scatter.39
  476.6 107.7 all-reduce.16
  592.1 79.0 reduce-scatter.41
  691.8 106.8 all-reduce.18
  803.8 79.1 reduce-scatter.43
  903.9 55.1 reduce-scatter.27
  987.3 106.9 all-reduce.20
  1096.9 58.3 reduce-scatter.29
  1183.6 106.9 all-reduce.22
  1293.9 58.3 reduce-scatter.31
  1381.8 107.1 all-reduce.24
  1491.3 58.4 reduce-scatter.33
  1579.4 106.9 all-reduce.26
  1689.2 58.5 reduce-scatter.35
where the time goes:
time: 1760 us
  waiting for transfers between devices  1460 us (83%)
  blocking collectives  190 us (11%)
  other arithmetic  54.8 us (3%)
  local copies, waits for them, and re-layouts  31.1 us (2%)
    psum x4, waiting for transfers between devices, tile_terms(): return lax.psum(local_terms, 'col')  432 us
    psum x4, waiting for transfers between devices, shards(): lax.psum(jnp.stack([leaf_part, upper_part]), 'col').astype(jnp.float32)  427 us
    unnamed x21, waiting for transfers between devices  315 us
    reduce_scatter x5, waiting for transfers between devices, backward_solve(): lax.psum_scatter(lax.cond(active, rows_compute, lambda: jnp.zeros((row_co...  287 us
    all_gather x5, blocking collectives, forward_solve(): shard_rows = lax.all_gather(shares, 'col', axis=0, tiled=True)  96 us
    all_gather x4, blocking collectives, fetch(): gathered = lax.all_gather(answer_up[None], 'leaf', axis=0, tiled=True)  94.3 us
  transfers between devices with their start and end apart: 17, of which 17 were waited for; matrix products, arithmetic and copies ran while one was open for 0% of the time, Pallas kernels for 0%

commit v1 on v0

--- a/solution.py
+++ b/solution.py
@@ -89,7 +89,9 @@
 
 def fetch(answer_up, height, leaf_id):
     owner = leaf_id // 2**height * 2**height + 2 ** (height - 1)
-    gathered = lax.all_gather(answer_up[None], "leaf", axis=0, tiled=True)
+    gathered = jnp.concatenate(
+        lax.all_to_all(jnp.stack([answer_up[None]] * lax.axis_size("leaf")), "leaf", 0, 0), axis=0
+    )
     return lax.dynamic_index_in_dim(gathered, owner, 0, keepdims=False)
 
 

time: 1760 us -> 1730 us (0.983)
  blocking collectives: 190 us -> 96 us
  waiting for transfers between devices: 1460 us -> 1490 us
  starting transfers between devices: 0.67 us -> 29.7 us
    all_gather x4 -> x0, blocking collectives: 94.3 us -> none  [fetch(): gathered = lax.all_gather(answer_up[None], 'leaf', axis=0, tiled=True)]
    all_to_all x0 -> x4, starting transfers between devices: none -> 29.1 us  [fetch(): lax.all_to_all(jnp.stack([answer_up[None]] * lax.axis_size('leaf')), 'lea...]
    all_to_all x0 -> x4, waiting for transfers between devices: none -> 25.8 us  [fetch(): lax.all_to_all(jnp.stack([answer_up[None]] * lax.axis_size('leaf')), 'lea...]
  transfers between devices with their start and end apart: 17 -> 21, of which waited for: 17 -> 21; matrix products, arithmetic and copies ran while one was open for 0% -> 0% of each run, Pallas kernels for 0% -> 0%
where the time goes in v1:
time: 1730 us
  waiting for transfers between devices  1490 us (86%)
  blocking collectives  96 us (6%)
  other arithmetic  54.8 us (3%)
  local copies, waits for them, and re-layouts  35.8 us (2%)
  starting transfers between devices  29.7 us (2%)
    psum x4, waiting for transfers between devices, tile_terms(): return lax.psum(local_terms, 'col')  432 us
    psum x4, waiting for transfers between devices, shards(): lax.psum(jnp.stack([leaf_part, upper_part]), 'col').astype(jnp.float32)  431 us
    unnamed x21, waiting for transfers between devices  315 us
    reduce_scatter x5, waiting for transfers between devices, backward_solve(): lax.psum_scatter(lax.cond(active, rows_compute, lambda: jnp.zeros((row_co...  289 us
    all_gather x5, blocking collectives, forward_solve(): shard_rows = lax.all_gather(shares, 'col', axis=0, tiled=True)  96 us
  transfers between devices with their start and end apart: 21, of which 21 were waited for; matrix products, arithmetic and copies ran while one was open for 0% of the time, Pallas kernels for 0%

profile of v1, /device:TPU:4, one launch (start us, length us, event | category | flops | bytes accessed | tf_op | source)
XLA Modules:
  0.0 1726.0 jit_solution(9505569677209155708)
XLA Ops:
  9.4 21.2 %all_gather.15 = bf16[1792,128]{1,0:T(8,128)(2,1)S(1)} all-gather(bf16[112,128]{1,0:T(8,128)(2,1)S(1)} %fusion.53), channel_id=1, replica_groups=mesh['leaf'=16,'col'=16] {'col'}, dimensions={0}, use_global_device_ids=true | all-gather | bytes 487424 | tf_op jit(solution)/shard_map/all_gather | solution.py:10
  34.5 108.2 %all-reduce.13.cloned.1.call-done = f32[4,512,128]{1,2,0:T(8,128)} async-done(((f32[4,512,128]{1,2,0:T(8,128)}), f32[4,512,128]{1,2,0:T(8,128)}) %all-reduce.13.cloned.1.call-update) | async-done | bytes 1048592 | tf_op jit(solution)/shard_map/psum | solution.py:28
  144.3 11.5 scatter_custom_fusion.1
  158.5 77.6 %reduce-scatter.38.cloned.1.call-done = f32[1,112,128]{2,1,0:T(8,128)} async-done(((f32[16,112,128]{2,1,0:T(8,128)}), f32[1,112,128]{2,1,0:T(8,128)}) %reduce-scatter.38.cloned.1.call-update) | async-done | bytes 57360
  237.0 18.7 %all_gather.16 = bf16[1792,128]{1,0:T(8,128)(2,1)S(1)} all-gather(bf16[112,128]{1,0:T(8,128)(2,1)S(1)} %multiply_convert_fusion.11), channel_id=1, replica_groups=mesh['leaf'=16,'col'=16] {'col'}, dimensions={0}, use_global_device_ids=true | all-gather | bytes 487424 | tf_op jit(solution)/shard_map/all_gather | solution.py:10
  257.0 109.0 %all-reduce.15.cloned.1.call-done = f32[3,512,128]{2,1,0:T(8,128)} async-done(((f32[3,512,128]{2,1,0:T(8,128)}), f32[3,512,128]{2,1,0:T(8,128)}) %all-reduce.15.cloned.1.call-update) | async-done | bytes 786448 | tf_op jit(solution)/shard_map/psum | solution.py:28
  366.0 9.1 scatter_custom_fusion.2
  377.1 78.3 %reduce-scatter.40.cloned.1.call-done = f32[1,112,128]{2,1,0:T(8,128)} async-done(((f32[16,112,128]{2,1,0:T(8,128)}), f32[1,112,128]{2,1,0:T(8,128)}) %reduce-scatter.40.cloned.1.call-update) | async-done | bytes 57360
  456.3 18.7 %all_gather.17 = bf16[1792,128]{1,0:T(8,128)(2,1)S(1)} all-gather(bf16[112,128]{1,0:T(8,128)(2,1)S(1)} %get-tuple-element.234), channel_id=1, replica_groups=mesh['leaf'=16,'col'=16] {'col'}, dimensions={0}, use_global_device_ids=true | all-gather | bytes 487424 | tf_op jit(solution)/shard_map/all_gather | solution.py:10
  476.6 107.9 %all-reduce.17.cloned.1.call-done = f32[2,512,128]{2,1,0:T(8,128)} async-done(((f32[2,512,128]{2,1,0:T(8,128)}), f32[2,512,128]{2,1,0:T(8,128)}) %all-reduce.17.cloned.1.call-update) | async-done | bytes 524304 | tf_op jit(solution)/shard_map/psum | solution.py:28
  584.5 6.4 scatter_custom_fusion.3
  592.1 79.1 %reduce-scatter.42.cloned.1.call-done = f32[1,112,128]{2,1,0:T(8,128)} async-done(((f32[16,112,128]{2,1,0:T(8,128)}), f32[1,112,128]{2,1,0:T(8,128)}) %reduce-scatter.42.cloned.1.call-update) | async-done | bytes 57360
  672.2 18.7 %all_gather.18 = bf16[1792,128]{1,0:T(8,128)(2,1)S(1)} all-gather(bf16[112,128]{1,0:T(8,128)(2,1)S(1)} %multiply_convert_fusion.7), channel_id=1, replica_groups=mesh['leaf'=16,'col'=16] {'col'}, dimensions={0}, use_global_device_ids=true | all-gather | bytes 487424 | tf_op jit(solution)/shard_map/all_gather | solution.py:10
  691.9 106.9 %all-reduce.19.cloned.1.call-done = f32[1,512,128]{2,1,0:T(8,128)} async-done(((f32[1,512,128]{2,1,0:T(8,128)}), f32[1,512,128]{2,1,0:T(8,128)}) %all-reduce.19.cloned.1.call-update) | async-done | bytes 262160 | tf_op jit(solution)/shard_map/psum | solution.py:28
  803.8 79.3 %reduce-scatter.44.cloned.1.call-done = f32[1,112,128]{2,1,0:T(8,128)} async-done(((f32[16,112,128]{2,1,0:T(8,128)}), f32[1,112,128]{2,1,0:T(8,128)}) %reduce-scatter.44.cloned.1.call-update) | async-done | bytes 57360
  884.0 18.7 %all_gather.19 = bf16[1792,128]{1,0:T(8,128)(2,1)S(1)} all-gather(bf16[112,128]{1,0:T(8,128)(2,1)S(1)} %fusion.55), channel_id=1, replica_groups=mesh['leaf'=16,'col'=16] {'col'}, dimensions={0}, use_global_device_ids=true | all-gather | bytes 487424 | tf_op jit(solution)/shard_map/all_gather | solution.py:10
  905.2 54.0 %reduce-scatter.28.cloned.1.call-done = f32[112,128]{1,0:T(8,128)} async-done(((f32[1792,128]{1,0:T(8,128)}), f32[112,128]{1,0:T(8,128)}) %reduce-scatter.28.cloned.1.call-update) | async-done | bytes 57360 | tf_op jit(solution)/shard_map/reduce_scatter | solution.py:63
  960.9 7.3 all-to-all-start
  969.4 5.9 all-to-all-done
  979.1 107.8 %all-reduce.21.cloned.1.call-done = bf16[2,512,128]{2,1,0:T(8,128)(2,1)} async-done(((bf16[2,512,128]{2,1,0:T(8,128)(2,1)}), bf16[2,512,128]{2,1,0:T(8,128)(2,1)}) %all-reduce.21.cloned.1.call-update) | async-done | bytes 262160 | tf_op jit(solution)/shard_map/psum | solution.py:157
  1089.1 58.7 %reduce-scatter.30.cloned.1.call-done = f32[112,128]{1,0:T(8,128)} async-done(((f32[1792,128]{1,0:T(8,128)}), f32[112,128]{1,0:T(8,128)}) %reduce-scatter.30.cloned.1.call-update) | async-done | bytes 57360 | tf_op jit(solution)/shard_map/reduce_scatter | solution.py:63
  1149.5 7.3 all-to-all-start.1
  1156.9 7.1 all-to-all-done.1
  1167.8 107.8 %all-reduce.23.cloned.1.call-done = bf16[2,512,128]{2,1,0:T(8,128)(2,1)} async-done(((bf16[2,512,128]{2,1,0:T(8,128)(2,1)}), bf16[2,512,128]{2,1,0:T(8,128)(2,1)}) %all-reduce.23.cloned.1.call-update) | async-done | bytes 262160 | tf_op jit(solution)/shard_map/psum | solution.py:157
  1278.8 58.5 %reduce-scatter.32.cloned.1.call-done = f32[112,128]{1,0:T(8,128)} async-done(((f32[1792,128]{1,0:T(8,128)}), f32[112,128]{1,0:T(8,128)}) %reduce-scatter.32.cloned.1.call-update) | async-done | bytes 57360 | tf_op jit(solution)/shard_map/reduce_scatter | solution.py:63
  1339.0 7.3 all-to-all-start.2
  1358.5 108.0 %all-reduce.25.cloned.1.call-done = bf16[2,512,128]{2,1,0:T(8,128)(2,1)} async-done(((bf16[2,512,128]{2,1,0:T(8,128)(2,1)}), bf16[2,512,128]{2,1,0:T(8,128)(2,1)}) %all-reduce.25.cloned.1.call-update) | async-done | bytes 262160 | tf_op jit(solution)/shard_map/psum | solution.py:157
  1468.4 58.9 %reduce-scatter.34.cloned.1.call-done = f32[112,128]{1,0:T(8,128)} async-done(((f32[1792,128]{1,0:T(8,128)}), f32[112,128]{1,0:T(8,128)}) %reduce-scatter.34.cloned.1.call-update) | async-done | bytes 57360 | tf_op jit(solution)/shard_map/reduce_scatter | solution.py:63
  1529.1 7.3 all-to-all-start.3
  1536.4 7.1 all-to-all-done.3
  1549.4 107.1 %all-reduce.27.cloned.1.call-done = bf16[2,512,128]{2,1,0:T(8,128)(2,1)} async-done(((bf16[2,512,128]{2,1,0:T(8,128)(2,1)}), bf16[2,512,128]{2,1,0:T(8,128)(2,1)}) %all-reduce.27.cloned.1.call-update) | async-done | bytes 262160 | tf_op jit(solution)/shard_map/psum | solution.py:157
  1659.3 58.7 %reduce-scatter.36.cloned.1.call-done = f32[112,128]{1,0:T(8,128)} async-done(((f32[1792,128]{1,0:T(8,128)}), f32[112,128]{1,0:T(8,128)}) %reduce-scatter.36.cloned.1.call-update) | async-done | bytes 57360 | tf_op jit(solution)/shard_map/reduce_scatter | solution.py:63
  (241 shorter events, 74.9 us)
Async XLA Ops:
  6.5 24.4 %copy-start = (bf16[1,4,112,512]{3,2,1,0:T(8,128)(2,1)S(1)}, bf16[1,4,112,512]{3,2,1,0:T(8,128)(2,1)}, u32[]{:S(2)}) copy-start(bf16[1,4,112,512]{3,2,1,0:T(8,128)(2,1)} %param.38) | copy-start | bytes 1376260
  6.5 24.1 %copy-start.8 = (bf16[1,112,1792]{2,1,0:T(8,128)(2,1)S(1)}, bf16[1,112,1792]{2,1,0:T(8,128)(2,1)}, u32[]{:S(2)}) copy-start(bf16[1,112,1792]{2,1,0:T(8,128)(2,1)} %param.36) | copy-start | bytes 1204228
  6.5 136.2 %all-reduce.13.cloned.1.call-start = ((), (), s32[]{:S(2)}) async-start(), calls=%async_computation.13 | async-start | bytes 2097152 | tf_op jit(solution)/shard_map/psum | solution.py:28
  32.3 203.8 %reduce-scatter.38.cloned.1.call-start = ((), (), s32[]{:S(2)}) async-start(), calls=%async_computation.26 | async-start | bytes 974848
  156.9 1.6 copy-start.10
  156.9 209.1 %all-reduce.15.cloned.1.call-start = ((), (), s32[]{:S(2)}) async-start(), calls=%async_computation.14 | async-start | bytes 1572864 | tf_op jit(solution)/shard_map/psum | solution.py:28
  158.5 77.6 %copy-start.24 = (bf16[1,2,112,128]{3,2,1,0:T(8,128)(2,1)S(1)}, bf16[1,2,112,128]{3,2,1,0:T(8,128)(2,1)}, u32[]{:S(2)}) copy-start(bf16[1,2,112,128]{3,2,1,0:T(8,128)(2,1)} %param.35) | copy-start | bytes 172036
  158.5 97.2 %copy-start.1 = (bf16[1,112,1792]{2,1,0:T(8,128)(2,1)S(1)}, bf16[1,112,1792]{2,1,0:T(8,128)(2,1)}, u32[]{:S(2)}) copy-start(bf16[1,112,1792]{2,1,0:T(8,128)(2,1)} %param.37) | copy-start | bytes 1204228
  256.8 198.6 %reduce-scatter.40.cloned.1.call-start = ((), (), s32[]{:S(2)}) async-start(), calls=%async_computation.27 | async-start | bytes 974848
  376.2 208.2 %all-reduce.17.cloned.1.call-start = ((), (), s32[]{:S(2)}) async-start(), calls=%async_computation.15 | async-start | bytes 1048576 | tf_op jit(solution)/shard_map/psum | solution.py:28
  377.1 78.4 %copy-start.20 = (f32[1,112,128]{2,1,0:T(8,128)S(1)}, f32[1,112,128]{2,1,0:T(8,128)}, u32[]{:S(2)}) copy-start(f32[1,112,128]{2,1,0:T(8,128)} %reduce-scatter.38.cloned.1.call-done) | copy-start | bytes 172036
  476.5 194.8 %reduce-scatter.42.cloned.1.call-start = ((), (), s32[]{:S(2)}) async-start(), calls=%async_computation.28 | async-start | bytes 974848
  592.0 206.7 %all-reduce.19.cloned.1.call-start = ((), (), s32[]{:S(2)}) async-start(), calls=%async_computation.16 | async-start | bytes 524288 | tf_op jit(solution)/shard_map/psum | solution.py:28
  691.8 191.4 %reduce-scatter.44.cloned.1.call-start = ((), (), s32[]{:S(2)}) async-start(), calls=%async_computation.29 | async-start | bytes 974848
  803.7 79.4 %copy-start.22 = (f32[1,112,128]{2,1,0:T(8,128)S(1)}, f32[1,112,128]{2,1,0:T(8,128)}, u32[]{:S(2)}) copy-start(f32[1,112,128]{2,1,0:T(8,128)} %reduce-scatter.42.cloned.1.call-done) | copy-start | bytes 172036
  803.8 155.4 %reduce-scatter.28.cloned.1.call-start = ((), (), s32[]{:S(2)}) async-start(), calls=%async_computation.21 | async-start | bytes 974848 | tf_op jit(solution)/shard_map/reduce_scatter | solution.py:63
  902.8 185.1 %copy-start.11 = (bf16[112,128]{1,0:T(8,128)(2,1)}, bf16[112,128]{1,0:T(8,128)(2,1)S(1)}, u32[]{:S(2)}) copy-start(bf16[112,128]{1,0:T(8,128)(2,1)S(1)} %get-tuple-element.233) | copy-start | bytes 86020
  960.9 14.4 all-to-all-start
  968.2 118.7 %all-reduce.21.cloned.1.call-start = ((), (), s32[]{:S(2)}) async-start(), calls=%async_computation.17 | async-start | bytes 524288 | tf_op jit(solution)/shard_map/psum | solution.py:157
  979.0 168.8 %reduce-scatter.30.cloned.1.call-start = ((), (), s32[]{:S(2)}) async-start(), calls=%async_computation.22 | async-start | bytes 974848 | tf_op jit(solution)/shard_map/reduce_scatter | solution.py:63
  1088.1 59.7 %copy-start.21 = (f32[112,128]{1,0:T(8,128)S(1)}, f32[112,128]{1,0:T(8,128)}, u32[]{:S(2)}) copy-start(f32[112,128]{1,0:T(8,128)} %reduce-scatter.28.cloned.1.call-done) | copy-start | bytes 172036
  1149.5 14.4 all-to-all-start.1
  1156.8 118.8 %all-reduce.23.cloned.1.call-start = ((), (), s32[]{:S(2)}) async-start(), calls=%async_computation.18 | async-start | bytes 524288 | tf_op jit(solution)/shard_map/psum | solution.py:157
  1167.7 169.5 %reduce-scatter.32.cloned.1.call-start = ((), (), s32[]{:S(2)}) async-start(), calls=%async_computation.23 | async-start | bytes 974848 | tf_op jit(solution)/shard_map/reduce_scatter | solution.py:63
  1277.8 59.5 %copy-start.19 = (bf16[112,128]{1,0:T(8,128)(2,1)S(1)}, bf16[112,128]{1,0:T(8,128)(2,1)}, u32[]{:S(2)}) copy-start(bf16[112,128]{1,0:T(8,128)(2,1)} %copy-done.18) | copy-start | bytes 86020
  1339.0 14.4 all-to-all-start.2
  1346.3 120.3 %all-reduce.25.cloned.1.call-start = ((), (), s32[]{:S(2)}) async-start(), calls=%async_computation.19 | async-start | bytes 524288 | tf_op jit(solution)/shard_map/psum | solution.py:157
  1358.4 168.9 %reduce-scatter.34.cloned.1.call-start = ((), (), s32[]{:S(2)}) async-start(), calls=%async_computation.24 | async-start | bytes 974848 | tf_op jit(solution)/shard_map/reduce_scatter | solution.py:63
  1529.1 14.4 all-to-all-start.3
  1536.4 120.2 %all-reduce.27.cloned.1.call-start = ((), (), s32[]{:S(2)}) async-start(), calls=%async_computation.20 | async-start | bytes 524288 | tf_op jit(solution)/shard_map/psum | solution.py:157
  1548.5 169.5 %reduce-scatter.36.cloned.1.call-start = ((), (), s32[]{:S(2)}) async-start(), calls=%async_computation.25 | async-start | bytes 974848 | tf_op jit(solution)/shard_map/reduce_scatter | solution.py:63
  1549.4 107.1 %copy-start.17 = (bf16[128,112]{0,1:T(8,128)(2,1)S(1)}, bf16[128,112]{0,1:T(8,128)(2,1)}, u32[]{:S(2)}) copy-start(bf16[128,112]{0,1:T(8,128)(2,1)} %copy-done.16) | copy-start | bytes 86020
  (25 other events, 19.9 us)
Sparse Core Ops, SparseCore 0:
  32.4 110.2 all-reduce.12
  157.1 78.9 reduce-scatter.37
  256.9 108.9 all-reduce.14
  376.4 79.0 reduce-scatter.39
  476.6 107.7 all-reduce.16
  592.2 79.0 reduce-scatter.41
  691.9 106.8 all-reduce.18
  803.9 79.1 reduce-scatter.43
  904.0 55.1 reduce-scatter.27
  979.1 107.6 all-reduce.20
  1089.4 58.3 reduce-scatter.29
  1167.8 107.7 all-reduce.22
  1278.9 58.3 reduce-scatter.31
  1358.6 107.8 all-reduce.24
  1468.9 58.4 reduce-scatter.33
  1548.6 107.8 all-reduce.26
  1659.4 58.5 reduce-scatter.35
